TPU v7x, 32 devices: a whole 2x2x4 slice. The times are simulated.
32 devices in a mesh: grp: 2 (over y), ep: 8 (over z, x), tp: 2 (over core).
Axes of the slice: x: 2, y: 2, z: 4, core: 2. Of those that a mesh axis runs over, the one named last changes fastest.
Arguments:
- queries: bfloat16 [1024, 16, 576], P(('grp', 'ep'), 'tp'), parts along dimension 0, may hold values from -450 to 450
- latent_cache: bfloat16 [48, 512, 576], P(('grp', 'ep'), 'tp'), parts along dimension 0, may hold values from -6 to 6
- residual: bfloat16 [1024, 2048], P(('grp', 'ep')), parts along dimension 0, may hold values from -8 to 8
- token_request: int32 [1024], P(('grp', 'ep')), parts along dimension 0, may hold values from 0 to 2, as said below
- token_visible: int32 [1024], P(('grp', 'ep')), parts along dimension 0, may hold values from 1 to 512, as said below
- value_proj: bfloat16 [16, 512, 128], P('tp', 'ep'), may hold values from -0.25 to 0.25
- out_proj: bfloat16 [2048, 2048], P('tp', 'ep'), may hold values from -0.125 to 0.125
- norm_gain: float32 [2048], replicated, may hold values from 0.1 to 1.9
- router: bfloat16 [2048, 64], replicated, may hold values from -0.0390625 to 0.0390625
- expert_ids: int32 [1024, 6], P(('grp', 'ep')), parts along dimension 0, may hold values from 0 to 63, all different within a row; in each aligned block of 64 rows (0 to 63, 64 to 127, ...) at most 8 rows name the same one
- gate_weight: bfloat16 [128, 2048, 384], P('ep', None, 'tp'), may hold values from -0.125 to 0.125
- up_weight: bfloat16 [128, 2048, 384], P('ep', None, 'tp'), may hold values from -0.125 to 0.125
- down_weight: bfloat16 [128, 384, 2048], P('ep', 'tp'), may hold values from -0.21875 to 0.21875
Outputs:
- hidden: bfloat16 [1024, 2048], P(('grp', 'ep'), 'tp'), parts along dimension 0
- expert_out: bfloat16 [1024, 2048], P(('grp', 'ep'), 'tp'), parts along dimension 0
There are 2 independent parts, one for each index of `grp`. A program takes and returns all parts, laid end to end along the dimension named above; an argument that names none is the same for every part. Nothing has to cross between parts.
Inputs may be any that keep to these rules, and one draw needn't show every extreme that they name: `token_request`: in each ep block, 62 tokens belong to request 0, a prefill span, and each other request has exactly one token; the tokens' order in the block is arbitrary. `token_visible`: the span's tokens read consecutive counts s + 1 to s + 62; 512 is reached in every draw. `expert_ids`: each row names 6 different experts; among the 64 tokens of one ep index no expert is named by more than 8 tokens, and this bound is reached.
All inputs are finite; a program needn't handle non-finite values.
Results may differ from a plain program's by a relative error of at most 0.018.
Values may be sent and summed in bfloat16 or wider, within the bound.
A program may use at most 128 MiB of HBM per device.

v0:
```python
import jax
import jax.numpy as jnp
from jax import lax
from jax.sharding import PartitionSpec as P

LATENT = 512
VDIM = 128
EXPERTS = 64
TOPK = 6
GROUPS = 2
CAP = 8
PIECES = 128
score_scale = 192.0 ** (-0.5)
epsilon = 1e-06


def masked_scores(queries, block_rows, token_request, token_visible):
    per_request = block_rows.shape[1]
    flat_rows = block_rows.reshape(-1, block_rows.shape[2])
    scores = (
        jnp.einsum("thc,kc->thk", queries, flat_rows, preferred_element_type=jnp.float32)
        * score_scale
    )
    column = jnp.arange(flat_rows.shape[0], dtype=jnp.int32)
    owner_id = column // per_request
    position = column % per_request
    allowed = (owner_id[None, :] == token_request[:, None]) & (
        position[None, :] < token_visible[:, None]
    )
    return (jnp.where(allowed[:, None, :], scores, -jnp.inf), flat_rows)


def weighted_rows(scores, row_peak, flat_rows):
    weights = jnp.exp(scores - row_peak[:, :, None]).astype(jnp.bfloat16)
    totals = jnp.sum(weights.astype(jnp.float32), axis=2)
    summed = jnp.einsum(
        "thk,kc->thc", weights, flat_rows[:, :LATENT], preferred_element_type=jnp.float32
    )
    return (summed, totals)


def expert_block(arrived, gate_weight, up_weight, down_weight):
    gate_vals = jnp.einsum("prd,pdf->prf", arrived, gate_weight, preferred_element_type=jnp.float32)
    up_vals = jnp.einsum("prd,pdf->prf", arrived, up_weight, preferred_element_type=jnp.float32)
    activated = (jax.nn.silu(gate_vals) * up_vals).astype(jnp.bfloat16)
    return jnp.einsum(
        "prf,pfd->prd", activated, down_weight, preferred_element_type=jnp.float32
    ).astype(jnp.bfloat16)


def body(
    queries,
    latent_cache,
    residual,
    token_request,
    token_visible,
    value_proj,
    out_proj,
    norm_gain,
    router,
    expert_ids,
    gate_weight,
    up_weight,
    down_weight,
):
    all_rows = lax.all_gather(latent_cache, "tp", axis=1, tiled=True)
    scores, flat_rows = masked_scores(queries, all_rows, token_request, token_visible)
    summed, totals = weighted_rows(scores, jnp.max(scores, axis=2), flat_rows)
    context = (summed / totals[:, :, None]).astype(jnp.bfloat16)
    tokens_here = context.shape[0]
    heads_here = context.shape[1]
    head_values = jnp.einsum(
        "thl,hlv->thv",
        context,
        lax.all_gather(value_proj, "ep", axis=1, tiled=True),
        preferred_element_type=jnp.float32,
    )
    heads_out = head_values.astype(jnp.bfloat16).reshape(tokens_here, heads_here * VDIM)
    column_block = jnp.dot(
        lax.all_gather(heads_out, "ep", axis=0, tiled=True),
        out_proj,
        preferred_element_type=jnp.float32,
    )
    attention_part = lax.all_to_all(column_block, "ep", split_axis=0, concat_axis=1, tiled=True)
    attention = lax.psum(attention_part, "tp")
    hidden = (residual.astype(jnp.float32) + attention).astype(jnp.bfloat16)
    hidden_wide = hidden.astype(jnp.float32)
    normed = (
        hidden_wide
        * lax.rsqrt(jnp.mean(hidden_wide * hidden_wide, axis=1, keepdims=True) + epsilon)
        * norm_gain
    ).astype(jnp.bfloat16)
    logits = jnp.dot(normed, router, preferred_element_type=jnp.float32)
    gate_share = jax.nn.softmax(jnp.take_along_axis(logits, expert_ids, axis=1), axis=1).astype(
        jnp.bfloat16
    )
    flat_ids = expert_ids.reshape(-1)
    position_id = jnp.arange(flat_ids.shape[0], dtype=jnp.int32)
    earlier = (flat_ids[:, None] == flat_ids[None, :]) & (
        position_id[None, :] < position_id[:, None]
    )
    slot_ids = (flat_ids * CAP + jnp.sum(earlier.astype(jnp.int32), axis=1)).reshape(
        tokens_here, TOPK
    )
    targets = jnp.arange(EXPERTS * CAP, dtype=jnp.int32)
    matches = slot_ids[:, :, None] == targets[None, None, :]
    picker = jnp.any(matches, axis=1).T.astype(jnp.bfloat16)
    model_width = normed.shape[1]
    mixing = jnp.sum(
        jnp.where(matches, gate_share[:, :, None], jnp.zeros((), jnp.bfloat16)), axis=1
    )
    mixing = jnp.broadcast_to(
        mixing.reshape(tokens_here, EXPERTS, 1, CAP), (tokens_here, EXPERTS, GROUPS, CAP)
    ).reshape(tokens_here, PIECES * CAP)
    core_count = lax.axis_size("tp")
    half_width = model_width // core_count
    core_start = lax.axis_index("tp") * half_width
    outgoing = jnp.dot(picker, normed, preferred_element_type=jnp.float32).astype(jnp.bfloat16)
    outgoing = jnp.broadcast_to(
        outgoing.reshape(EXPERTS, 1, CAP, model_width), (EXPERTS, GROUPS, CAP, model_width)
    ).reshape(PIECES, CAP, model_width)
    arrived = lax.all_to_all(outgoing, "ep", split_axis=0, concat_axis=1, tiled=True)
    partial_out = expert_block(arrived, gate_weight, up_weight, down_weight)
    returned = lax.all_to_all(partial_out, "ep", split_axis=1, concat_axis=0, tiled=True)
    routed = jnp.dot(
        mixing, returned.reshape(PIECES * CAP, model_width), preferred_element_type=jnp.float32
    )
    expert_out = lax.psum_scatter(
        routed.astype(jnp.bfloat16), "tp", scatter_dimension=1, tiled=True
    )
    hidden_part = lax.dynamic_slice_in_dim(hidden, core_start, half_width, 1)
    return (hidden_part, expert_out)


def solution(mesh):
    return jax.shard_map(
        body,
        mesh=mesh,
        in_specs=(
            P(("grp", "ep"), "tp", None),
            P(("grp", "ep"), "tp", None),
            P(("grp", "ep"), None),
            P(("grp", "ep")),
            P(("grp", "ep")),
            P("tp", "ep", None),
            P("tp", "ep"),
            P(),
            P(),
            P(("grp", "ep"), None),
            P("ep", None, "tp"),
            P("ep", None, "tp"),
            P("ep", "tp", None),
        ),
        out_specs=(P(("grp", "ep"), "tp"), P(("grp", "ep"), "tp")),
        check_vma=False,
    )
```

profile of v0, /device:TPU:0, one launch (start us, length us, event | category | flops | bytes accessed | tf_op | source)
XLA Modules:
  0.0 395.9 jit_solution(957612986233958496)
XLA Ops:
  8.7 0.8 compare_and_fusion
  9.6 12.4 %all-gather.4.cloned.1.call-done = bf16[3,512,576]{1,2,0:T(8,128)(2,1)} async-done(((bf16[3,256,576]{1,2,0:T(8,128)(2,1)}), bf16[3,512,576]{1,2,0:T(8,128)(2,1)}) %all-gather.4.cloned.1.call-update) | async-done | bytes 1769488 | tf_op jit(solution)/shard_map/all_gather | solution.py:66
  22.0 2.7 copy.88
  24.7 3.2 convert_reduce_fusion
  28.0 37.6 %all-gather.6.cloned.1.call-done = bf16[8,512,128]{2,1,0:T(8,128)(2,1)} async-done(((bf16[8,64,128]{2,1,0:T(8,128)(2,1)}), bf16[8,512,128]{2,1,0:T(8,128)(2,1)}) %all-gather.6.cloned.1.call-update) | async-done | bytes 1048592 | tf_op jit(solution)/shard_map/all_gather | solution.py:75
  65.6 2.9 fusion.22
  69.3 39.1 %all-gather.8.cloned.1.call-done = bf16[512,1024]{1,0:T(8,128)(2,1)} async-done(((bf16[64,1024]{1,0:T(8,128)(2,1)}), bf16[512,1024]{1,0:T(8,128)(2,1)}) %all-gather.8.cloned.1.call-update) | async-done | bytes 1048592 | tf_op jit(solution)/shard_map/all_gather | solution.py:80
  108.4 1.7 fusion.54
  110.1 15.7 %all_to_all.52 = f32[8,64,256]{2,1,0:T(8,128)S(1)} all-to-all(f32[8,64,256]{2,1,0:T(8,128)S(1)} %bitcast.65), channel_id=1, replica_groups=mesh['grp'=2,'ep'=8,'tp'=2] {'ep'}, dimensions={0} | all-to-all | bytes 1048576 | tf_op jit(solution)/shard_map/all_to_all | solution.py:84
  125.8 0.9 copy.107
  127.6 16.9 %all-reduce.2.cloned.1.call-done = f32[64,2048]{1,0:T(8,128)} async-done(((f32[64,2048]{1,0:T(8,128)}), f32[64,2048]{1,0:T(8,128)}) %all-reduce.2.cloned.1.call-update) | async-done | bytes 524304 | tf_op jit(solution)/shard_map/psum | solution.py:85
  144.5 1.2 fusion.35
  145.8 0.8 fusion.11
  147.1 99.2 %all_to_all.53 = bf16[128,8,2048]{2,1,0:T(8,128)(2,1)S(1)} all-to-all(bf16[128,8,2048]{2,1,0:T(8,128)(2,1)S(1)} %bitcast.62), channel_id=1, replica_groups=mesh['grp'=2,'ep'=8,'tp'=2] {'ep'}, dimensions={0} | all-to-all | bytes 8388608 | tf_op jit(solution)/shard_map/all_to_all | solution.py:122
  246.3 2.0 copy-done.2
  248.3 10.0 %fusion.3 = f32[16,64,192]{2,1,0:T(8,128)} fusion(bf16[16,2048,192]{1,2,0:T(8,128)(2,1)} %param.23, bf16[16,8,8,2048]{3,2,0,1:T(8,128)(2,1)S(1)} %bitcast.59), kind=kOutput, calls=%fused_computation.4 | convolution fusion | flops 805306368 | bytes 17563648 | tf_op jit(solution)/shard_map/prd,pdf->prf/dot_general | solution.py:43
  258.2 14.3 %convolution_convert_fusion = bf16[16,64,2048]{2,1,0:T(8,128)(2,1)} fusion(bf16[16,192,2048]{2,1,0:T(8,128)(2,1)} %param.25, bf16[16,2048,192]{1,2,0:T(8,128)(2,1)} %param.24, bf16[16,8,8,2048]{3,2,0,1:T(8,128)(2,1)} %bitcast.60, f32[16,64,192]{2,1,0:T(8,128)} %fusion.3), kind=kOutput, calls=%fused_computation.7 | convolution fusion | flops 1613889536 | bytes 34340864 | tf_op jit(solution)/shard_map/prf,pfd->prd/dot_general | solution.py:46
  272.5 6.5 %copy.100 = bf16[16,64,2048]{2,0,1:T(8,128)(2,1)} copy(bf16[16,64,2048]{2,1,0:T(8,128)(2,1)} %convolution_convert_fusion) | data formatting | bytes 8388608 | tf_op jit(solution)/shard_map/convert_element_type | solution.py:48
  279.0 4.7 %all-to-all-start.2 = ((bf16[16,64,2048]{2,0,1:T(8,128)(2,1)}), bf16[16,64,2048]{2,0,1:T(8,128)(2,1)}, u32[]{:S(2)}, u32[]{:S(2)}) async-start(bf16[16,64,2048]{2,0,1:T(8,128)(2,1)} %copy.100), calls=%async_computation.2 | async-start | bytes 8388608 | tf_op jit(solution)/shard_map/all_to_all | solution.py:124
  284.5 2.9 gather_fusion
  288.0 88.1 %all-to-all-done.2 = bf16[16,64,2048]{2,0,1:T(8,128)(2,1)} async-done(((bf16[16,64,2048]{2,0,1:T(8,128)(2,1)}), bf16[16,64,2048]{2,0,1:T(8,128)(2,1)}, u32[]{:S(2)}, u32[]{:S(2)}) %all-to-all-start.2) | async-done | bytes 4194336 | tf_op jit(solution)/shard_map/all_to_all | solution.py:124
  376.1 4.7 %copy.102 = bf16[8,16,8,2048]{3,2,1,0:T(8,128)(2,1)S(1)} copy(bf16[8,16,8,2048]{3,1,2,0:T(8,128)(2,1)} %bitcast.16) | data formatting | bytes 8388608 | tf_op jit(solution)/shard_map/all_to_all | solution.py:124
  380.8 1.6 convolution_convert_fusion.2
  383.1 6.2 %reduce-scatter.2.cloned.1.call-done = bf16[64,1024]{1,0:T(8,128)(2,1)} async-done(((bf16[64,2048]{1,0:T(8,128)(2,1)}), bf16[64,1024]{1,0:T(8,128)(2,1)}) %reduce-scatter.2.cloned.1.call-update) | async-done | bytes 131088 | tf_op jit(solution)/shard_map/reduce_scatter | solution.py:128
  (50 shorter events, 5.9 us)
Async XLA Ops:
  7.2 17.6 %copy-start = (bf16[64,8,576]{2,1,0:T(8,128)(2,1)S(1)}, bf16[64,8,576]{2,1,0:T(8,128)(2,1)}, u32[]{:S(2)}) copy-start(bf16[64,8,576]{2,1,0:T(8,128)(2,1)} %param.13) | copy-start | bytes 1769476
  7.2 14.8 %all-gather.4.cloned.1.call-start = ((), (), s32[]{:S(2)}) async-start(), calls=%async_computation.4 | async-start | bytes 2654208 | tf_op jit(solution)/shard_map/all_gather | solution.py:66
  7.9 57.7 %all-gather.6.cloned.1.call-start = ((), (), s32[]{:S(2)}) async-start(), calls=%async_computation.5 | async-start | bytes 1179648 | tf_op jit(solution)/shard_map/all_gather | solution.py:75
  8.7 99.8 %all-gather.8.cloned.1.call-start = ((), (), s32[]{:S(2)}) async-start(), calls=%async_computation.6 | async-start | bytes 1179648 | tf_op jit(solution)/shard_map/all_gather | solution.py:80
  65.6 42.8 %copy-start.3 = (bf16[1024,256]{1,0:T(8,128)(2,1)S(1)}, bf16[1024,256]{1,0:T(8,128)(2,1)}, u32[]{:S(2)}) copy-start(bf16[1024,256]{1,0:T(8,128)(2,1)} %param.19) | copy-start | bytes 1572868
  68.5 58.2 %copy-start.5 = (s32[64,6]{0,1:T(8,128)S(1)}, s32[64,6]{0,1:T(8,128)}, u32[]{:S(2)}) copy-start(s32[64,6]{0,1:T(8,128)} %param.22) | copy-start | bytes 4612
  68.6 76.0 %copy-start.4 = (bf16[64,2048]{1,0:T(8,128)(2,1)S(1)}, bf16[64,2048]{1,0:T(8,128)(2,1)}, u32[]{:S(2)}) copy-start(bf16[64,2048]{1,0:T(8,128)(2,1)} %param.15) | copy-start | bytes 786436
  68.6 77.2 %copy-start.6 = (f32[2048]{0:T(1024)S(1)}, f32[2048]{0:T(1024)}, u32[]{:S(2)}) copy-start(f32[2048]{0:T(1024)} %param.20) | copy-start | bytes 24580
  69.3 75.2 %all-reduce.2.cloned.1.call-start = ((), (), s32[]{:S(2)}) async-start(), calls=%async_computation.7 | async-start | bytes 1048576 | tf_op jit(solution)/shard_map/psum | solution.py:85
  246.3 2.0 copy-start.2
  279.0 5.2 %copy-start.7 = (bf16[2048,64]{0,1:T(8,128)(2,1)S(1)}, bf16[2048,64]{0,1:T(8,128)(2,1)}, u32[]{:S(2)}) copy-start(bf16[2048,64]{0,1:T(8,128)(2,1)} %param.21) | copy-start | bytes 786436
  279.0 97.1 %all-to-all-start.2 = ((bf16[16,64,2048]{2,0,1:T(8,128)(2,1)}), bf16[16,64,2048]{2,0,1:T(8,128)(2,1)}, u32[]{:S(2)}, u32[]{:S(2)}) async-start(bf16[16,64,2048]{2,0,1:T(8,128)(2,1)} %copy.100), calls=%async_computation.2 | async-start | bytes 8388608 | tf_op jit(solution)/shard_map/all_to_all | solution.py:124
  283.7 105.7 %reduce-scatter.2.cloned.1.call-start = ((), (), s32[]{:S(2)}) async-start(), calls=%async_computation.8 | async-start | bytes 393216 | tf_op jit(solution)/shard_map/reduce_scatter | solution.py:128
  376.1 13.2 %copy-start.1 = (bf16[64,8,576]{2,1,0:T(8,128)(2,1)S(1)}, bf16[64,8,576]{2,1,0:T(8,128)(2,1)}, u32[]{:S(2)}) copy-start(bf16[64,8,576]{2,1,0:T(8,128)(2,1)} %param.13) | copy-start | bytes 1769476
Sparse Core Ops, SparseCore 0:
  9.5 12.4 all-gather.3
  24.2 41.4 all-gather.5
  69.4 38.9 all-gather.7
  126.8 17.6 all-reduce.1
  382.5 6.7 reduce-scatter.1
where the time goes:
time: 396 us
  waiting for transfers between devices  202 us (51%)
  blocking collectives  115 us (29%)
  matrix products  34.7 us (9%)
  local copies, waits for them, and re-layouts  22.6 us (6%)
  between operations  14 us (4%)
  starting transfers between devices  5.09 us (1%)
    all_to_all x1, blocking collectives, body(): lax.all_to_all(outgoing, 'ep', split_axis=0, concat_axis=1, tiled=True)  99.2 us
    all_to_all x1, waiting for transfers between devices, body(): lax.all_to_all(partial_out, 'ep', split_axis=1, concat_axis=0, tiled=True)  88.1 us
    all_gather x1, waiting for transfers between devices, body(): lax.all_gather(heads_out, 'ep', axis=0, tiled=True)  39.1 us
    all_gather x1, waiting for transfers between devices, body(): lax.all_gather(value_proj, 'ep', axis=1, tiled=True)  37.6 us
    psum x1, waiting for transfers between devices, body(): attention = lax.psum(attention_part, 'tp')  16.9 us
    all_to_all x1, blocking collectives, body(): lax.all_to_all(column_block, 'ep', split_axis=0, concat_axis=1, tiled=True)  15.7 us
    dot_general x1, matrix products, expert_block(): jnp.einsum('prf,pfd->prd', activated, down_weight, preferred_element_type...  14.3 us
    all_gather x1, waiting for transfers between devices, body(): all_rows = lax.all_gather(latent_cache, 'tp', axis=1, tiled=True)  12.4 us
  transfers between devices with their start and end apart: 6, of which 6 were waited for; matrix products, arithmetic and copies ran while one was open for 3% of the time, Pallas kernels for 0%

commit v1 on v0

--- a/solution.py
+++ b/solution.py
@@ -69,12 +69,37 @@
     context = (summed / totals[:, :, None]).astype(jnp.bfloat16)
     tokens_here = context.shape[0]
     heads_here = context.shape[1]
+    size, mine, rows = (lax.axis_size("ep"), lax.axis_index("ep"), value_proj.shape[1])
+    ahead = [(i, (i + 1) % size) for i in range(size)]
+    behind = [(i, (i - 1) % size) for i in range(size)]
+    half = size // 2
+    from_left = from_right = value_proj
     head_values = jnp.einsum(
         "thl,hlv->thv",
-        context,
-        lax.all_gather(value_proj, "ep", axis=1, tiled=True),
+        lax.dynamic_slice_in_dim(context, mine * rows, value_proj.shape[1], axis=2),
+        value_proj,
         preferred_element_type=jnp.float32,
     )
+    for step in range(1, half + 1):
+        from_left = lax.ppermute(from_left, "ep", ahead)
+        if step < size - half:
+            from_right = lax.ppermute(from_right, "ep", behind)
+            head_values = head_values + jnp.einsum(
+                "thl,hlv->thv",
+                lax.dynamic_slice_in_dim(
+                    context, (mine + step) % size * rows, from_right.shape[1], axis=2
+                ),
+                from_right,
+                preferred_element_type=jnp.float32,
+            )
+        head_values = head_values + jnp.einsum(
+            "thl,hlv->thv",
+            lax.dynamic_slice_in_dim(
+                context, (mine - step) % size * rows, from_left.shape[1], axis=2
+            ),
+            from_left,
+            preferred_element_type=jnp.float32,
+        )
     heads_out = head_values.astype(jnp.bfloat16).reshape(tokens_here, heads_here * VDIM)
     column_block = jnp.dot(
         lax.all_gather(heads_out, "ep", axis=0, tiled=True),

time: 396 us -> 376 us (0.949)
  waiting for transfers between devices: 202 us -> 162 us
  starting transfers between devices: 5.09 us -> 21.7 us
    all_gather x1 -> x0, waiting for transfers between devices: 37.6 us -> none  [body(): lax.all_gather(value_proj, 'ep', axis=1, tiled=True)]
    ppermute x0 -> x7, starting transfers between devices: none -> 16.7 us  [the longest x3 9.74 us: body(): from_right = lax.ppermute(from_right, 'ep', behind)]
    all_gather x1, waiting for transfers between devices: 12.4 us -> 0.01 us  [body(): all_rows = lax.all_gather(latent_cache, 'tp', axis=1, tiled=True)]
    ppermute x0 -> x7, waiting for transfers between devices: none -> 8.5 us  [the longest x4 8.49 us: body(): from_left = lax.ppermute(from_left, 'ep', ahead)]
  transfers between devices with their start and end apart: 6 -> 12, of which waited for: 6 -> 7; matrix products, arithmetic and copies ran while one was open for 3% -> 5% of each run, Pallas kernels for 0% -> 0%
where the time goes in v1:
time: 376 us; the launch traced here: 375 us
  waiting for transfers between devices  162 us (43%)
  blocking collectives  115 us (31%)
  matrix products  36.5 us (10%)
  local copies, waits for them, and re-layouts  22.9 us (6%)
  starting transfers between devices  21.7 us (6%)
  between operations  14.2 us (4%)
    all_to_all x1, blocking collectives, body(): lax.all_to_all(outgoing, 'ep', split_axis=0, concat_axis=1, tiled=True)  99.2 us
    all_to_all x1, waiting for transfers between devices, body(): lax.all_to_all(partial_out, 'ep', split_axis=1, concat_axis=0, tiled=True)  88.1 us
    all_gather x1, waiting for transfers between devices, body(): lax.all_gather(heads_out, 'ep', axis=0, tiled=True)  41.6 us
    psum x1, waiting for transfers between devices, body(): attention = lax.psum(attention_part, 'tp')  16.9 us
    all_to_all x1, blocking collectives, body(): lax.all_to_all(column_block, 'ep', split_axis=0, concat_axis=1, tiled=True)  15.7 us
    dot_general x1, matrix products, expert_block(): jnp.einsum('prf,pfd->prd', activated, down_weight, preferred_element_type...  14.3 us
    dot_general x1, matrix products, expert_block(): jnp.einsum('prd,pdf->prf', arrived, gate_weight, preferred_element_type=j...  9.93 us
    ppermute x3, starting transfers between devices, body(): from_right = lax.ppermute(from_right, 'ep', behind)  9.74 us
  transfers between devices with their start and end apart: 12, of which 7 were waited for; matrix products, arithmetic and copies ran while one was open for 5% of the time, Pallas kernels for 0%

profile of v1, /device:TPU:0, one launch (start us, length us, event | category | flops | bytes accessed | tf_op | source)
XLA Modules:
  0.0 375.0 jit_solution(8934345797703294140)
XLA Ops:
  8.0 3.0 collective-permute-start.1
  11.0 3.1 collective-permute-start
  14.1 3.7 collective-permute-done.1
  19.2 3.5 collective-permute-start.2
  22.8 2.7 collective-permute-done.3
  25.5 1.7 collective-permute-start.5
  28.1 3.1 collective-permute-start.4
  31.2 2.0 collective-permute-done.5
  34.1 2.7 copy.123
  36.8 3.2 convert_reduce_fusion
  40.1 2.4 fusion.23
  46.0 41.6 %all-gather.5.cloned.1.call-done = bf16[512,1024]{1,0:T(8,128)(2,1)} async-done(((bf16[64,1024]{1,0:T(8,128)(2,1)}), bf16[512,1024]{1,0:T(8,128)(2,1)}) %all-gather.5.cloned.1.call-update) | async-done | bytes 1048592 | tf_op jit(solution)/shard_map/all_gather | solution.py:105
  89.3 15.7 %all_to_all.52 = f32[8,64,256]{2,1,0:T(8,128)S(1)} all-to-all(f32[8,64,256]{2,1,0:T(8,128)S(1)} %bitcast.73), channel_id=1, replica_groups=mesh['grp'=2,'ep'=8,'tp'=2] {'ep'}, dimensions={0} | all-to-all | bytes 1048576 | tf_op jit(solution)/shard_map/all_to_all | solution.py:109
  106.8 16.9 %all-reduce.2.cloned.1.call-done = f32[64,2048]{1,0:T(8,128)} async-done(((f32[64,2048]{1,0:T(8,128)}), f32[64,2048]{1,0:T(8,128)}) %all-reduce.2.cloned.1.call-update) | async-done | bytes 524304 | tf_op jit(solution)/shard_map/psum | solution.py:110
  126.2 99.2 %all_to_all.53 = bf16[128,8,2048]{2,1,0:T(8,128)(2,1)S(1)} all-to-all(bf16[128,8,2048]{2,1,0:T(8,128)(2,1)S(1)} %bitcast.70), channel_id=1, replica_groups=mesh['grp'=2,'ep'=8,'tp'=2] {'ep'}, dimensions={0} | all-to-all | bytes 8388608 | tf_op jit(solution)/shard_map/all_to_all | solution.py:147
  225.4 2.0 copy-done.2
  227.4 9.9 %fusion.2 = f32[16,64,192]{2,1,0:T(8,128)} fusion(bf16[16,2048,192]{1,2,0:T(8,128)(2,1)} %param.23, bf16[16,8,8,2048]{3,2,0,1:T(8,128)(2,1)S(1)} %bitcast.67), kind=kOutput, calls=%fused_computation.3 | convolution fusion | flops 805306368 | bytes 17563648 | tf_op jit(solution)/shard_map/prd,pdf->prf/dot_general | solution.py:43
  237.3 14.3 %convolution_convert_fusion = bf16[16,64,2048]{2,1,0:T(8,128)(2,1)} fusion(bf16[16,192,2048]{2,1,0:T(8,128)(2,1)} %param.25, bf16[16,2048,192]{1,2,0:T(8,128)(2,1)} %param.24, bf16[16,8,8,2048]{3,2,0,1:T(8,128)(2,1)} %bitcast.68, f32[16,64,192]{2,1,0:T(8,128)} %fusion.2), kind=kOutput, calls=%fused_computation.5 | convolution fusion | flops 1613889536 | bytes 34340864 | tf_op jit(solution)/shard_map/prf,pfd->prd/dot_general | solution.py:46
  251.6 6.4 %copy.141 = bf16[16,64,2048]{2,0,1:T(8,128)(2,1)} copy(bf16[16,64,2048]{2,1,0:T(8,128)(2,1)} %convolution_convert_fusion) | data formatting | bytes 8388608 | tf_op jit(solution)/shard_map/convert_element_type | solution.py:48
  258.1 4.7 %all-to-all-start.2 = ((bf16[16,64,2048]{2,0,1:T(8,128)(2,1)}), bf16[16,64,2048]{2,0,1:T(8,128)(2,1)}, u32[]{:S(2)}, u32[]{:S(2)}) async-start(bf16[16,64,2048]{2,0,1:T(8,128)(2,1)} %copy.141), calls=%async_computation.2 | async-start | bytes 8388608 | tf_op jit(solution)/shard_map/all_to_all | solution.py:149
  263.6 2.9 gather_fusion
  267.1 88.1 %all-to-all-done.2 = bf16[16,64,2048]{2,0,1:T(8,128)(2,1)} async-done(((bf16[16,64,2048]{2,0,1:T(8,128)(2,1)}), bf16[16,64,2048]{2,0,1:T(8,128)(2,1)}, u32[]{:S(2)}, u32[]{:S(2)}) %all-to-all-start.2) | async-done | bytes 4194336 | tf_op jit(solution)/shard_map/all_to_all | solution.py:149
  355.2 4.7 %copy.143 = bf16[8,16,8,2048]{3,2,1,0:T(8,128)(2,1)S(1)} copy(bf16[8,16,8,2048]{3,1,2,0:T(8,128)(2,1)} %bitcast.16) | data formatting | bytes 8388608 | tf_op jit(solution)/shard_map/all_to_all | solution.py:149
  362.2 6.2 %reduce-scatter.2.cloned.1.call-done = bf16[64,1024]{1,0:T(8,128)(2,1)} async-done(((bf16[64,2048]{1,0:T(8,128)(2,1)}), bf16[64,1024]{1,0:T(8,128)(2,1)}) %reduce-scatter.2.cloned.1.call-update) | async-done | bytes 131088 | tf_op jit(solution)/shard_map/reduce_scatter | solution.py:153
  (71 shorter events, 16.8 us)
Async XLA Ops:
  7.2 29.7 %copy-start = (bf16[64,8,576]{2,1,0:T(8,128)(2,1)S(1)}, bf16[64,8,576]{2,1,0:T(8,128)(2,1)}, u32[]{:S(2)}) copy-start(bf16[64,8,576]{2,1,0:T(8,128)(2,1)} %param.13) | copy-start | bytes 1769476
  7.2 26.9 %all-gather.3.cloned.1.call-start = ((), (), s32[]{:S(2)}) async-start(), calls=%async_computation.4 | async-start | bytes 2654208 | tf_op jit(solution)/shard_map/all_gather | solution.py:66
  7.9 79.7 %all-gather.5.cloned.1.call-start = ((), (), s32[]{:S(2)}) async-start(), calls=%async_computation.5 | async-start | bytes 1179648 | tf_op jit(solution)/shard_map/all_gather | solution.py:105
  8.0 9.9 %collective-permute-start.1 = (bf16[8,64,128]{2,1,0:T(8,128)(2,1)}, bf16[8,64,128]{2,1,0:T(8,128)(2,1)S(1)}, u32[]{:S(2)}, u32[]{:S(2)}) collective-permute-start(bf16[8,64,128]{2,1,0:T(8,128)(2,1)} %param.18), channel_id=1, source_target_pairs={{0,2},{2,4},{4,6},{6,8},{8,10},{10,12},{12,14},{14,0},{1,3},{3,5},... | collective-permute-start | bytes 393224 | tf_op jit(solution)/shard_map/ppermute | solution.py:84
  11.0 8.3 %collective-permute-start = (bf16[8,64,128]{2,1,0:T(8,128)(2,1)}, bf16[8,64,128]{2,1,0:T(8,128)(2,1)S(1)}, u32[]{:S(2)}, u32[]{:S(2)}) collective-permute-start(bf16[8,64,128]{2,1,0:T(8,128)(2,1)} %param.18), channel_id=1, source_target_pairs={{0,14},{2,0},{4,2},{6,4},{8,6},{10,8},{12,10},{14,12},{1,15},{3,1}... | collective-permute-start | bytes 393224 | tf_op jit(solution)/shard_map/ppermute | solution.py:86
  17.8 7.7 %collective-permute-start.3 = (bf16[8,64,128]{2,1,0:T(8,128)(2,1)S(1)}, bf16[8,64,128]{2,1,0:T(8,128)(2,1)S(1)}, u32[]{:S(2)}, u32[]{:S(2)}) collective-permute-start(bf16[8,64,128]{2,1,0:T(8,128)(2,1)S(1)} %collective-permute-done.1), channel_id=1, source_target_pairs={{0,2},{2,4},{4,6},{6,8},{8,10},{10,12},{12,14},{14,0},{1,3},{3,5},... | collective-permute-start | bytes 393224 | tf_op jit(solution)/shard_map/ppermute | solution.py:84
  19.2 8.9 %collective-permute-start.2 = (bf16[8,64,128]{2,1,0:T(8,128)(2,1)S(1)}, bf16[8,64,128]{2,1,0:T(8,128)(2,1)S(1)}, u32[]{:S(2)}, u32[]{:S(2)}) collective-permute-start(bf16[8,64,128]{2,1,0:T(8,128)(2,1)S(1)} %collective-permute-done), channel_id=1, source_target_pairs={{0,14},{2,0},{4,2},{6,4},{8,6},{10,8},{12,10},{14,12},{1,15},{3,1}... | collective-permute-start | bytes 393224 | tf_op jit(solution)/shard_map/ppermute | solution.py:86
  25.5 7.8 %collective-permute-start.5 = (bf16[8,64,128]{2,1,0:T(8,128)(2,1)S(1)}, bf16[8,64,128]{2,1,0:T(8,128)(2,1)S(1)}, u32[]{:S(2)}, u32[]{:S(2)}) collective-permute-start(bf16[8,64,128]{2,1,0:T(8,128)(2,1)S(1)} %collective-permute-done.3), channel_id=1, source_target_pairs={{0,2},{2,4},{4,6},{6,8},{8,10},{10,12},{12,14},{14,0},{1,3},{3,5},... | collective-permute-start | bytes 393224 | tf_op jit(solution)/shard_map/ppermute | solution.py:84
  28.1 15.9 %collective-permute-start.4 = (bf16[8,64,128]{2,1,0:T(8,128)(2,1)S(1)}, bf16[8,64,128]{2,1,0:T(8,128)(2,1)}, u32[]{:S(2)}, u32[]{:S(2)}) collective-permute-start(bf16[8,64,128]{2,1,0:T(8,128)(2,1)S(1)} %collective-permute-done.2), channel_id=1, source_target_pairs={{0,14},{2,0},{4,2},{6,4},{8,6},{10,8},{12,10},{14,12},{1,15},{3,1}... | collective-permute-start | bytes 393224 | tf_op jit(solution)/shard_map/ppermute | solution.py:86
  33.3 11.8 %collective-permute-start.6 = (bf16[8,64,128]{2,1,0:T(8,128)(2,1)S(1)}, bf16[8,64,128]{2,1,0:T(8,128)(2,1)S(1)}, u32[]{:S(2)}, u32[]{:S(2)}) collective-permute-start(bf16[8,64,128]{2,1,0:T(8,128)(2,1)S(1)} %collective-permute-done.5), channel_id=1, source_target_pairs={{0,2},{2,4},{4,6},{6,8},{8,10},{10,12},{12,14},{14,0},{1,3},{3,5},... | collective-permute-start | bytes 393224 | tf_op jit(solution)/shard_map/ppermute | solution.py:84
  40.1 2.8 copy-start.6
  42.5 45.1 %copy-start.3 = (bf16[1024,256]{1,0:T(8,128)(2,1)S(1)}, bf16[1024,256]{1,0:T(8,128)(2,1)}, u32[]{:S(2)}) copy-start(bf16[1024,256]{1,0:T(8,128)(2,1)} %param.19) | copy-start | bytes 1572868
  43.6 62.3 %copy-start.5 = (s32[64,6]{0,1:T(8,128)S(1)}, s32[64,6]{0,1:T(8,128)}, u32[]{:S(2)}) copy-start(s32[64,6]{0,1:T(8,128)} %param.22) | copy-start | bytes 4612
  43.6 80.0 %copy-start.4 = (bf16[64,2048]{1,0:T(8,128)(2,1)S(1)}, bf16[64,2048]{1,0:T(8,128)(2,1)}, u32[]{:S(2)}) copy-start(bf16[64,2048]{1,0:T(8,128)(2,1)} %param.15) | copy-start | bytes 786436
  43.8 81.1 %copy-start.7 = (f32[2048]{0:T(1024)S(1)}, f32[2048]{0:T(1024)}, u32[]{:S(2)}) copy-start(f32[2048]{0:T(1024)} %param.20) | copy-start | bytes 24580
  46.0 77.7 %all-reduce.2.cloned.1.call-start = ((), (), s32[]{:S(2)}) async-start(), calls=%async_computation.6 | async-start | bytes 1048576 | tf_op jit(solution)/shard_map/psum | solution.py:110
  225.4 2.0 copy-start.2
  258.1 5.2 %copy-start.8 = (bf16[2048,64]{0,1:T(8,128)(2,1)S(1)}, bf16[2048,64]{0,1:T(8,128)(2,1)}, u32[]{:S(2)}) copy-start(bf16[2048,64]{0,1:T(8,128)(2,1)} %param.21) | copy-start | bytes 786436
  258.1 97.1 %all-to-all-start.2 = ((bf16[16,64,2048]{2,0,1:T(8,128)(2,1)}), bf16[16,64,2048]{2,0,1:T(8,128)(2,1)}, u32[]{:S(2)}, u32[]{:S(2)}) async-start(bf16[16,64,2048]{2,0,1:T(8,128)(2,1)} %copy.141), calls=%async_computation.2 | async-start | bytes 8388608 | tf_op jit(solution)/shard_map/all_to_all | solution.py:149
  262.8 105.7 %reduce-scatter.2.cloned.1.call-start = ((), (), s32[]{:S(2)}) async-start(), calls=%async_computation.7 | async-start | bytes 393216 | tf_op jit(solution)/shard_map/reduce_scatter | solution.py:153
  355.2 13.2 %copy-start.1 = (bf16[64,8,576]{2,1,0:T(8,128)(2,1)S(1)}, bf16[64,8,576]{2,1,0:T(8,128)(2,1)}, u32[]{:S(2)}) copy-start(bf16[64,8,576]{2,1,0:T(8,128)(2,1)} %param.13) | copy-start | bytes 1769476
Sparse Core Ops, SparseCore 0:
  9.5 12.4 all-gather.2
  46.1 41.4 all-gather.4
  106.0 17.6 all-reduce.1
  361.6 6.7 reduce-scatter.1
